TPU v7x, 32 devices: a whole 2x2x4 slice. The times are simulated.
32 devices in a mesh: rep: 8 (over z, y), tp: 4 (over x, core).
Axes of the slice: x: 2, y: 2, z: 4, core: 2. Of those that a mesh axis runs over, the one named last changes fastest.
Arguments:
- image_grads: bfloat16 [32, 48, 1280], P('rep', 'tp'), may hold values from -6 to 6
- dest_rank: int32 [32], P('rep'), may hold values from 0 to 7, as said below
- dest_slot: int32 [32], P('rep'), may hold values from 0 to 7, as said below
- saved_inputs: bfloat16 [64, 48, 1280], P('rep'), may hold values from -6 to 6
- up_weight: bfloat16 [1280, 5120], P(None, 'tp'), may hold values from -0.15625 to 0.15625
- down_weight: bfloat16 [5120, 1280], P('tp'), may hold values from -0.078125 to 0.078125
- norm_gain: float32 [1280], replicated, may hold values from 0.25 to 1.75
Outputs:
- input_grads: bfloat16 [64, 48, 1280], P('rep', 'tp')
- up_grads: float32 [1280, 5120], P('rep', 'tp')
- down_grads: float32 [5120, 1280], P('tp', 'rep')
- gain_grads: float32 [1280], replicated
Inputs may be any that keep to these rules, and one draw needn't show every extreme that they name: `dest_rank`: the images of one index of rep go to different owners; each owner receives at most 8 images, and some owner receives exactly 8 in every draw. `dest_slot`: the images that one owner receives have distinct slots 0, 1, ... up to their count less one; other slots hold no image.
All inputs are finite; a program needn't handle non-finite values.
Results may differ from a plain program's by a relative error of at most 0.015.
Values may be sent and summed in bfloat16 or wider, within the bound.
No kernel may reach another device: no remote copies, remote signals or barrier semaphores. Data moves between devices by JAX's collectives and lax.ppermute only.
A program may use at most 128 MiB of HBM per device.

v0:
```python
import jax
import jax.numpy as jnp
from jax import lax
from jax.sharding import PartitionSpec as P

epsilon = 1e-05
gelu_c = 0.7978845608028654
gelu_a = 0.044715


def gelu_value(preact):
    inner = jnp.tanh(gelu_c * (preact + gelu_a * preact**3))
    return 0.5 * preact * (1.0 + inner)


def gelu_slope(preact):
    inner = jnp.tanh(gelu_c * (preact + gelu_a * preact**3))
    return 0.5 * (1.0 + inner) + 0.5 * preact * (1.0 - inner * inner) * gelu_c * (
        1.0 + 3.0 * gelu_a * preact * preact
    )


def outbound(images, dest_rank, dest_slot, groups, capacity):
    rank_ids = jnp.arange(groups, dtype=jnp.int32)
    one_hot = dest_rank[None, :] == rank_ids[:, None]
    packed = jnp.einsum(
        "ek,kpd->epd", one_hot.astype(jnp.bfloat16), images, preferred_element_type=jnp.float32
    ).astype(jnp.bfloat16)
    present = jnp.any(one_hot, axis=1)
    slot_sent = jnp.sum(jnp.where(one_hot, dest_slot[None, :], 0), axis=1) + jnp.where(
        present, 0, capacity
    )
    return (packed, slot_sent)


def compact(inbound, slot_recv, capacity):
    slot_ids = jnp.arange(capacity, dtype=jnp.int32)
    picker = (slot_recv[None, :] == slot_ids[:, None]).astype(jnp.bfloat16)
    return jnp.einsum("ce,epd->cpd", picker, inbound, preferred_element_type=jnp.float32).astype(
        jnp.bfloat16
    )


def local(image_grads, dest_rank, dest_slot, saved_inputs, up_weight, down_weight, norm_gain):
    groups = lax.axis_size("rep")
    capacity = saved_inputs.shape[0]
    patches = saved_inputs.shape[1]
    width = saved_inputs.shape[2]
    slab = image_grads.shape[1]
    packed, slot_sent = outbound(image_grads, dest_rank, dest_slot, groups, capacity)
    inbound, slot_recv = (
        lax.all_to_all(packed, "rep", split_axis=0, concat_axis=0, tiled=True),
        lax.all_to_all(slot_sent, "rep", split_axis=0, concat_axis=0, tiled=True),
    )
    routed = lax.all_gather(compact(inbound, slot_recv, capacity), "tp", axis=1, tiled=True)
    rows = capacity * patches
    grads = routed.reshape(rows, width)
    values = saved_inputs.reshape(rows, width).astype(jnp.float32)
    mean_v = jnp.mean(values, axis=1, keepdims=True)
    var_v = jnp.mean((values - mean_v) ** 2, axis=1, keepdims=True)
    inv_std = 1.0 / jnp.sqrt(var_v + epsilon)
    centred = (values - mean_v) * inv_std
    normed = (centred * norm_gain[None, :]).astype(jnp.bfloat16)
    preact = jnp.dot(normed, up_weight, preferred_element_type=jnp.float32)
    hidden = gelu_value(preact).astype(jnp.bfloat16)
    grad_hidden = jnp.dot(grads, down_weight.T, preferred_element_type=jnp.float32)
    grad_pre = (grad_hidden * gelu_slope(preact)).astype(jnp.bfloat16)
    down_local = jnp.dot(hidden.T, grads, preferred_element_type=jnp.float32)
    up_local = jnp.dot(normed.T, grad_pre, preferred_element_type=jnp.float32)
    partial_normed = jnp.dot(grad_pre, up_weight.T, preferred_element_type=jnp.float32)
    up_grads, down_grads = (
        lax.psum_scatter(
            up_local.astype(jnp.bfloat16), "rep", scatter_dimension=0, tiled=True
        ).astype(jnp.float32),
        lax.psum_scatter(
            down_local.astype(jnp.bfloat16), "rep", scatter_dimension=1, tiled=True
        ).astype(jnp.float32),
    )
    start = lax.axis_index("tp") * slab
    grad_normed = lax.psum(partial_normed.astype(jnp.bfloat16), "tp").astype(jnp.float32)
    gain_grads = lax.psum(jnp.sum(grad_normed * centred, axis=0), "rep")
    scaled = grad_normed * norm_gain[None, :]
    first = jnp.mean(scaled, axis=1, keepdims=True)
    second = jnp.mean(scaled * centred, axis=1, keepdims=True)
    result = grads.astype(jnp.float32) + inv_std * (scaled - first - centred * second)
    result = result.reshape(capacity, patches, width)
    input_grads = lax.dynamic_slice_in_dim(result, start, slab, 1).astype(jnp.bfloat16)
    return (input_grads, up_grads, down_grads, gain_grads)


def solution(mesh):
    in_specs = (
        P("rep", "tp", None),
        P("rep"),
        P("rep"),
        P("rep", None, None),
        P(None, "tp"),
        P("tp", None),
        P(),
    )
    out_specs = (P("rep", "tp", None), P("rep", "tp"), P("tp", "rep"), P())
    return jax.shard_map(local, mesh=mesh, in_specs=in_specs, out_specs=out_specs, check_vma=False)
```

profile of v0, /device:TPU:0, one launch (start us, length us, event | category | flops | bytes accessed | tf_op | source)
XLA Modules:
  0.0 227.4 jit_solution(4812168266985921151)
XLA Ops:
  8.0 0.0 copy-start
  8.0 0.0 copy-start.6
  8.0 0.0 copy-start.4
  8.0 0.0 copy-start.5
  8.0 0.9 fusion.26
  8.9 0.9 select_reduce_fusion
  9.9 0.7 copy.19
  10.5 7.3 %all-to-all-start = ((s32[8,1,1]{2,1,0:T(1,128)}), s32[8,1,1]{2,1,0:T(1,128)S(1)}, u32[]{:S(2)}, u32[]{:S(2)}) async-start(s32[8,1,1]{2,1,0:T(1,128)} %copy.19), calls=%async_computation | async-start | bytes 8192 | tf_op jit(solution)/shard_map/all_to_all | solution.py:53
  17.8 1.4 convert_reduce_fusion
  19.3 0.1 div.18
  19.3 1.6 multiply_reduce_fusion
  20.9 0.1 sqrt.6
  21.0 0.0 copy-done.6
  21.0 0.0 copy-done.4
  21.1 0.3 convolution_convert_fusion.4
  21.4 0.0 copy-done.5
  21.4 2.5 %multiply_convert_fusion.1 = bf16[384,1280]{1,0:T(8,128)(2,1)} fusion(bf16[8,48,1280]{2,1,0:T(8,128)(2,1)} %param.10, f32[1280]{0:T(1024)S(1)} %copy-done.5, f32[384]{0:T(512)S(1)} %div.18, f32[384]{0:T(512)S(1)} %sqrt.6), kind=kLoop, calls=%fused_computation.29 | loop fusion | flops 2457600 | bytes 1974272 | tf_op jit(solution)/shard_map/convert_element_type | solution.py:63
  23.9 0.8 copy.20
  24.7 0.0 all-to-all-done
  24.7 6.0 %all-to-all-start.1 = ((bf16[8,12,1280]{2,1,0:T(8,128)(2,1)}), bf16[8,12,1280]{2,1,0:T(8,128)(2,1)}, u32[]{:S(2)}, u32[]{:S(2)}) async-start(bf16[8,12,1280]{2,1,0:T(8,128)(2,1)} %copy.20), calls=%async_computation.1 | async-start | bytes 655360 | tf_op jit(solution)/shard_map/all_to_all | solution.py:52
  30.7 0.0 all-reduce.2.cloned.1.call-start
  30.7 0.0 copy-done
  30.7 4.0 %fusion.33 = f32[384,1280]{1,0:T(8,128)} fusion(bf16[384,1280]{1,0:T(8,128)(2,1)} %multiply_convert_fusion.1, bf16[1280,1280]{1,0:T(8,128)(2,1)S(1)} %copy-done), kind=kOutput, calls=%fused_computation.56 | convolution fusion | flops 1258291200 | bytes 6225920 | tf_op jit(solution)/shard_map/dot_general | solution.py:64
  34.7 0.2 reduce.2
  34.9 5.6 %all-to-all-done.1 = bf16[8,12,1280]{2,1,0:T(8,128)(2,1)} async-done(((bf16[8,12,1280]{2,1,0:T(8,128)(2,1)}), bf16[8,12,1280]{2,1,0:T(8,128)(2,1)}, u32[]{:S(2)}, u32[]{:S(2)}) %all-to-all-start.1) | async-done | bytes 245792 | tf_op jit(solution)/shard_map/all_to_all | solution.py:52
  40.5 0.0 copy-start.7
  40.5 1.3 convolution_convert_fusion.3
  41.9 9.7 %all_gather.3 = bf16[8,48,1280]{2,0,1:T(8,128)(2,1)S(1)} all-gather(bf16[8,12,1280]{2,0,1:T(8,128)(2,1)S(1)} %convolution_convert_fusion.3), channel_id=1, replica_groups=mesh['rep'=8,'tp'=4] {'tp'}, dimensions={1}, use_global_device_ids=true | all-gather | bytes 1228800 | tf_op jit(solution)/shard_map/all_gather | solution.py:55
  51.5 0.2 copy.22
  51.7 0.0 copy-start.2
  51.7 0.0 copy-done.7
  51.7 3.8 %fusion = bf16[384,1280]{1,0:T(8,128)(2,1)S(1)} fusion(bf16[384,1280]{1,0:T(8,128)(2,1)S(1)} %bitcast.33, bf16[1280,1280]{1,0:T(8,128)(2,1)S(1)} %copy-done.7, f32[384,1280]{1,0:T(8,128)} %fusion.33), kind=kOutput, calls=%fused_computation.5 | convolution fusion | flops 1267630080 | bytes 7208960 | tf_op jit(solution)/shard_map/dot_general | solution.py:66
  55.5 0.0 copy-done.2
  55.6 0.0 copy-start.8
  55.6 0.9 copy-done.8
  56.5 2.4 %convolution_convert_fusion.2 = bf16[384,1280]{1,0:T(8,128)(2,1)} fusion(bf16[384,1280]{1,0:T(8,128)(2,1)S(1)} %fusion, bf16[1280,1280]{1,0:T(8,128)(2,1)S(1)} %copy-done), kind=kOutput, calls=%fused_computation.6 | convolution fusion | flops 1258782720 | bytes 5242880 | tf_op jit(solution)/shard_map/dot_general | solution.py:70
  58.9 0.0 all-reduce.2.cloned.1.call-update
  59.0 0.0 reduce-scatter.3.cloned.1.call-start
  59.0 5.1 %convolution_convert_fusion.1 = bf16[1280,1280]{1,0:T(8,128)(2,1)} fusion(bf16[384,1280]{1,0:T(8,128)(2,1)} %multiply_convert_fusion.1, bf16[384,1280]{1,0:T(8,128)(2,1)} %copy-done.8), kind=kOutput, calls=%fused_computation.1 | convolution fusion | flops 1259929600 | bytes 5242880 | tf_op jit(solution)/shard_map/dot_general | solution.py:69
  64.1 0.0 reduce-scatter.3.cloned.1.call-update
  64.1 0.2 reduce-scatter.5.cloned.1.call-start
  64.4 5.5 %convolution_convert_fusion = bf16[1280,1280]{0,1:T(8,128)(2,1)} fusion(bf16[384,1280]{1,0:T(8,128)(2,1)} %bitcast.34, f32[384,1280]{1,0:T(8,128)} %fusion.33), kind=kOutput, calls=%fused_computation | convolution fusion | flops 1264353280 | bytes 6225920 | tf_op jit(solution)/shard_map/dot_general | solution.py:68
  69.9 0.0 reduce-scatter.5.cloned.1.call-update
  69.9 23.6 %all-reduce.2.cloned.1.call-done = bf16[384,1280]{1,0:T(8,128)(2,1)} async-done(((bf16[384,1280]{1,0:T(8,128)(2,1)}), bf16[384,1280]{1,0:T(8,128)(2,1)}) %all-reduce.2.cloned.1.call-update) | async-done | bytes 983056 | tf_op jit(solution)/shard_map/psum | solution.py:80
  93.5 0.0 copy-start.1
  93.5 0.0 copy-start.3
  93.5 2.6 %fusion.8 = (f32[1280]{0:T(1024)S(1)}, f32[384]{0:T(512)S(1)}, f32[384]{0:T(512)S(1)}) fusion(bf16[384,1280]{1,0:T(8,128)(2,1)} %all-reduce.2.cloned.1.call-done, bf16[8,48,1280]{2,1,0:T(8,128)(2,1)} %param.10, f32[384]{0:T(512)S(1)} %div.18, f32[384]{0:T(512)S(1)} %sqrt.6, f32[1280]{0:T(1024)S(1)} %copy-done.5), kind=kLoop, calls=%fused_computation.18 | loop fusion | flops 4913152 | bytes 1982464 | tf_op jit(solution)/shard_map/reduce_sum | solution.py:81
  96.1 0.0 copy-done.1
  96.1 0.0 copy-done.3
  96.1 2.1 fusion.6
  98.2 0.1 constant_dynamic-slice_fusion
  98.3 0.8 copy.28
  99.0 22.1 %psum.15 = f32[1280]{0:T(1024)} all-reduce(f32[1280]{0:T(1024)S(1)} %get-tuple-element.4), channel_id=1, replica_groups=mesh['rep'=8,'tp'=4] {'rep'}, use_global_device_ids=true, to_apply=%region_10.11 | all-reduce | flops 1280 | bytes 10240 | tf_op jit(solution)/shard_map/psum | solution.py:81
  121.2 18.0 %reduce-scatter.3.cloned.1.call-done = bf16[160,1280]{1,0:T(8,128)(2,1)} async-done(((bf16[1280,1280]{1,0:T(8,128)(2,1)}), bf16[160,1280]{1,0:T(8,128)(2,1)}) %reduce-scatter.3.cloned.1.call-update) | async-done | bytes 409616 | tf_op jit(solution)/shard_map/reduce_scatter | solution.py:72
  139.2 1.9 convert_element_type.63
  141.1 76.9 %reduce-scatter.5.cloned.1.call-done = bf16[1280,160]{0,1:T(8,128)(2,1)} async-done(((bf16[1280,1280]{0,1:T(8,128)(2,1)}), bf16[1280,160]{0,1:T(8,128)(2,1)}) %reduce-scatter.5.cloned.1.call-update) | async-done | bytes 409616 | tf_op jit(solution)/shard_map/reduce_scatter | solution.py:75
  218.0 1.9 convert_element_type.66
  (4 shorter events, 0.0 us)
Async XLA Ops:
  8.0 22.7 %copy-start = (bf16[1280,1280]{1,0:T(8,128)(2,1)S(1)}, bf16[1280,1280]{1,0:T(8,128)(2,1)}, u32[]{:S(2)}) copy-start(bf16[1280,1280]{1,0:T(8,128)(2,1)} %param.11) | copy-start | bytes 9830404
  8.0 13.0 %copy-start.6 = (s32[4]{0:T(128)S(1)}, s32[4]{0:T(128)}, u32[]{:S(2)}) copy-start(s32[4]{0:T(128)} %param.8) | copy-start | bytes 52
  8.0 13.0 %copy-start.4 = (bf16[4,12,1280]{2,0,1:T(4,128)(2,1)S(1)}, bf16[4,12,1280]{2,0,1:T(4,128)(2,1)}, u32[]{:S(2)}) copy-start(bf16[4,12,1280]{2,0,1:T(4,128)(2,1)} %param.7) | copy-start | bytes 368644
  8.0 13.4 %copy-start.5 = (f32[1280]{0:T(1024)S(1)}, f32[1280]{0:T(1024)}, u32[]{:S(2)}) copy-start(f32[1280]{0:T(1024)} %param.13) | copy-start | bytes 15364
  10.5 14.2 %all-to-all-start = ((s32[8,1,1]{2,1,0:T(1,128)}), s32[8,1,1]{2,1,0:T(1,128)S(1)}, u32[]{:S(2)}, u32[]{:S(2)}) async-start(s32[8,1,1]{2,1,0:T(1,128)} %copy.19), calls=%async_computation | async-start | bytes 8192 | tf_op jit(solution)/shard_map/all_to_all | solution.py:53
  24.7 15.8 %all-to-all-start.1 = ((bf16[8,12,1280]{2,1,0:T(8,128)(2,1)}), bf16[8,12,1280]{2,1,0:T(8,128)(2,1)}, u32[]{:S(2)}, u32[]{:S(2)}) async-start(bf16[8,12,1280]{2,1,0:T(8,128)(2,1)} %copy.20), calls=%async_computation.1 | async-start | bytes 655360 | tf_op jit(solution)/shard_map/all_to_all | solution.py:52
  30.7 62.8 %all-reduce.2.cloned.1.call-start = ((), (), s32[]{:S(2)}) async-start(), calls=%async_computation.4 | async-start | bytes 1966080 | tf_op jit(solution)/shard_map/psum | solution.py:80
  40.5 11.2 %copy-start.7 = (bf16[1280,1280]{1,0:T(8,128)(2,1)S(1)}, bf16[1280,1280]{1,0:T(8,128)(2,1)}, u32[]{:S(2)}) copy-start(bf16[1280,1280]{1,0:T(8,128)(2,1)} %param.12) | copy-start | bytes 9830404
  51.7 3.9 %copy-start.2 = (bf16[8,48,1280]{2,1,0:T(8,128)(2,1)}, bf16[8,48,1280]{2,1,0:T(8,128)(2,1)S(1)}, u32[]{:S(2)}) copy-start(bf16[8,48,1280]{2,1,0:T(8,128)(2,1)S(1)} %copy.22) | copy-start | bytes 2949124
  55.6 1.0 copy-start.8
  59.0 80.2 %reduce-scatter.3.cloned.1.call-start = ((), (), s32[]{:S(2)}) async-start(), calls=%async_computation.5 | async-start | bytes 3686400 | tf_op jit(solution)/shard_map/reduce_scatter | solution.py:72
  64.1 153.9 %reduce-scatter.5.cloned.1.call-start = ((), (), s32[]{:S(2)}) async-start(), calls=%async_computation.6 | async-start | bytes 3686400 | tf_op jit(solution)/shard_map/reduce_scatter | solution.py:75
  93.5 2.6 %copy-start.1 = (bf16[8,48,1280]{2,1,0:T(8,128)(2,1)S(1)}, bf16[8,48,1280]{2,1,0:T(8,128)(2,1)}, u32[]{:S(2)}) copy-start(bf16[8,48,1280]{2,1,0:T(8,128)(2,1)} %param.10) | copy-start | bytes 2949124
  93.5 2.6 %copy-start.3 = (bf16[8,48,1280]{2,1,0:T(8,128)(2,1)S(1)}, bf16[8,48,1280]{2,1,0:T(8,128)(2,1)}, u32[]{:S(2)}) copy-start(bf16[8,48,1280]{2,1,0:T(8,128)(2,1)} %copy-done.2) | copy-start | bytes 2949124
Sparse Core Ops, SparseCore 0:
  59.1 34.3 all-reduce.1
Sparse Core Ops, SparseCore 1:
  64.2 74.9 reduce-scatter.2
  142.6 75.3 reduce-scatter.4
where the time goes:
time: 228 us; the launch traced here: 227 us
  waiting for transfers between devices  124 us (54%)
  blocking collectives  31.8 us (14%)
  matrix products  22.5 us (10%)
  other arithmetic  16.1 us (7%)
  between operations  15.7 us (7%)
  starting transfers between devices  13.6 us (6%)
  local copies, waits for them, and re-layouts  3.62 us (2%)
    reduce_scatter x1, waiting for transfers between devices, local(): lax.psum_scatter(down_local.astype(jnp.bfloat16), 'rep', scatter_dimensio...  76.9 us
    psum x1, waiting for transfers between devices, local(): lax.psum(partial_normed.astype(jnp.bfloat16), 'tp').astype(jnp.float32)  23.6 us
    psum x1, blocking collectives, local(): gain_grads = lax.psum(jnp.sum(grad_normed * centred, axis=0), 'rep')  22.1 us
    reduce_scatter x1, waiting for transfers between devices, local(): lax.psum_scatter(up_local.astype(jnp.bfloat16), 'rep', scatter_dimension=...  18 us
    all_gather x1, blocking collectives, local(): lax.all_gather(compact(inbound, slot_recv, capacity), 'tp', axis=1, tiled...  9.67 us
    all_to_all x1, starting transfers between devices, local(): lax.all_to_all(slot_sent, 'rep', split_axis=0, concat_axis=0, tiled=True)  7.31 us
    all_to_all x1, starting transfers between devices, local(): lax.all_to_all(packed, 'rep', split_axis=0, concat_axis=0, tiled=True)  6 us
    all_to_all x1, waiting for transfers between devices, local(): lax.all_to_all(packed, 'rep', split_axis=0, concat_axis=0, tiled=True)  5.58 us
  transfers between devices with their start and end apart: 5, of which 4 were waited for; matrix products, arithmetic and copies ran while one was open for 13% of the time, Pallas kernels for 0%

commit v1 on v0

--- a/solution.py
+++ b/solution.py
@@ -42,6 +42,29 @@
 
 
 def local(image_grads, dest_rank, dest_slot, saved_inputs, up_weight, down_weight, norm_gain):
+
+    def _apply_tiles(local_values):
+        n_now, current_arr = (lax.axis_size("rep"), lax.axis_index("rep"))
+        all_values = list(local_values.shape)
+        y_new = local_values.shape[0] // n_now
+        all_values[0] = y_new
+        v_now = all_values[0]
+        all_values[0] = v_now * n_now
+        step_out = jnp.zeros(all_values, local_values.dtype)
+        for src_i in tuple(range(n_now)):
+            q_next = lax.dynamic_slice_in_dim(
+                local_values, (current_arr ^ src_i) * y_new, y_new, axis=0
+            )
+            if src_i:
+                row_list = []
+                for dev_i in tuple(range(n_now)):
+                    row_list.append((dev_i, dev_i ^ src_i))
+                q_next = lax.ppermute(q_next, "rep", row_list)
+            step_out = lax.dynamic_update_slice_in_dim(
+                step_out, q_next, (current_arr ^ src_i) * v_now, axis=0
+            )
+        return step_out
+
     groups = lax.axis_size("rep")
     capacity = saved_inputs.shape[0]
     patches = saved_inputs.shape[1]
@@ -50,7 +73,7 @@
     packed, slot_sent = outbound(image_grads, dest_rank, dest_slot, groups, capacity)
     inbound, slot_recv = (
         lax.all_to_all(packed, "rep", split_axis=0, concat_axis=0, tiled=True),
-        lax.all_to_all(slot_sent, "rep", split_axis=0, concat_axis=0, tiled=True),
+        _apply_tiles(slot_sent),
     )
     routed = lax.all_gather(compact(inbound, slot_recv, capacity), "tp", axis=1, tiled=True)
     rows = capacity * patches

time: 228 us -> 233 us (1.022)
  starting transfers between devices: 13.6 us -> 19.3 us
  local copies, waits for them, and re-layouts: 3.62 us -> 8.78 us
  waiting for transfers between devices: 124 us -> 119 us
    ppermute x0 -> x7, starting transfers between devices: none -> 14.1 us  [_apply_tiles(): q_next = lax.ppermute(q_next, 'rep', row_list)]
    all_to_all x1 -> x0, starting transfers between devices: 7.31 us -> none  [local(): lax.all_to_all(slot_sent, 'rep', split_axis=0, concat_axis=0, tiled=True)]
    all_to_all x1, waiting for transfers between devices: 5.58 us -> 0.01 us  [local(): lax.all_to_all(packed, 'rep', split_axis=0, concat_axis=0, tiled=True)]
    dynamic_update_slice x0 -> x7, local copies, waits for them, and re-layouts: none -> 5.08 us  [_apply_tiles(): lax.dynamic_update_slice_in_dim(step_out, q_next, (current_arr ^ src_i) *...]
  transfers between devices with their start and end apart: 5 -> 11, of which waited for: 4 -> 4; matrix products, arithmetic and copies ran while one was open for 13% -> 14% of each run, Pallas kernels for 0% -> 0%
where the time goes in v1:
time: 233 us; the launch traced here: 232 us
  waiting for transfers between devices  119 us (51%)
  blocking collectives  31.8 us (14%)
  matrix products  22.2 us (10%)
  starting transfers between devices  19.3 us (8%)
  between operations  15.7 us (7%)
  other arithmetic  14.8 us (6%)
  local copies, waits for them, and re-layouts  8.78 us (4%)
    reduce_scatter x1, waiting for transfers between devices, local(): lax.psum_scatter(down_local.astype(jnp.bfloat16), 'rep', scatter_dimensio...  76.7 us
    psum x1, waiting for transfers between devices, local(): lax.psum(partial_normed.astype(jnp.bfloat16), 'tp').astype(jnp.float32)  23 us
    psum x1, blocking collectives, local(): gain_grads = lax.psum(jnp.sum(grad_normed * centred, axis=0), 'rep')  22.1 us
    reduce_scatter x1, waiting for transfers between devices, local(): lax.psum_scatter(up_local.astype(jnp.bfloat16), 'rep', scatter_dimension=...  18.1 us
    ppermute x7, starting transfers between devices, _apply_tiles(): q_next = lax.ppermute(q_next, 'rep', row_list)  14.1 us
    all_gather x1, blocking collectives, local(): lax.all_gather(compact(inbound, slot_recv, capacity), 'tp', axis=1, tiled...  9.67 us
    dot_general x1, matrix products, local(): down_local = jnp.dot(hidden.T, grads, preferred_element_type=jnp.float32)  5.52 us
    dot_general x1, matrix products, local(): up_local = jnp.dot(normed.T, grad_pre, preferred_element_type=jnp.float32)  5.09 us
  transfers between devices with their start and end apart: 11, of which 4 were waited for; matrix products, arithmetic and copies ran while one was open for 14% of the time, Pallas kernels for 0%

profile of v1, /device:TPU:0, one launch (start us, length us, event | category | flops | bytes accessed | tf_op | source)
XLA Modules:
  0.0 231.8 jit_solution(4553498923756590631)
XLA Ops:
  8.0 0.0 copy-start
  8.1 0.9 fusion.26
  8.9 0.8 select_reduce_fusion
  9.8 0.8 fusion.33
  10.6 3.0 %collective-permute-start = (s32[1]{0:T(128)}, s32[1]{0:T(128)}, u32[]{:S(2)}, u32[]{:S(2)}) collective-permute-start(s32[1]{0:T(128)} %get-tuple-element.13), channel_id=1, source_target_pairs={{0,4},{4,0},{8,12},{12,8},{16,20},{20,16},{24,28},{28,24},{1,5},{5... | collective-permute-start | bytes 20 | tf_op jit(solution)/shard_map/ppermute | solution.py:62
  13.6 1.6 collective-permute-start.1
  15.1 0.0 collective-permute-start.2
  15.1 3.0 %collective-permute-start.3 = (s32[1]{0:T(128)}, s32[1]{0:T(128)}, u32[]{:S(2)}, u32[]{:S(2)}) collective-permute-start(s32[1]{0:T(128)} %get-tuple-element.10), channel_id=1, source_target_pairs={{0,16},{4,20},{8,24},{12,28},{16,0},{20,4},{24,8},{28,12},{1,17},{... | collective-permute-start | bytes 20 | tf_op jit(solution)/shard_map/ppermute | solution.py:62
  18.1 1.3 collective-permute-start.4
  19.4 1.2 convolution_convert_fusion.4
  20.7 0.8 copy.14
  21.4 4.9 %all-to-all-start = ((bf16[8,12,1280]{2,1,0:T(8,128)(2,1)}), bf16[8,12,1280]{2,1,0:T(8,128)(2,1)}, u32[]{:S(2)}, u32[]{:S(2)}) async-start(bf16[8,12,1280]{2,1,0:T(8,128)(2,1)} %copy.14), calls=%async_computation | async-start | bytes 655360 | tf_op jit(solution)/shard_map/all_to_all | solution.py:75
  26.3 0.0 all-reduce.2.cloned.1.call-start
  26.3 1.4 convert_reduce_fusion
  27.8 1.6 multiply_reduce_fusion
  29.4 0.1 div.18
  29.5 0.1 sqrt.6
  29.5 0.0 copy-done.5
  29.5 1.6 multiply_convert_fusion.1
  31.1 0.0 copy-done
  31.1 0.0 copy-start.4
  31.1 2.8 %fusion.34 = f32[384,1280]{1,0:T(8,128)} fusion(bf16[384,1280]{1,0:T(8,128)(2,1)S(1)} %multiply_convert_fusion.1, bf16[1280,1280]{1,0:T(8,128)(2,1)S(1)} %copy-done), kind=kOutput, calls=%fused_computation.58 | convolution fusion | flops 1258291200 | bytes 6225920 | tf_op jit(solution)/shard_map/dot_general | solution.py:87
  33.9 0.0 collective-permute-done
  33.9 3.8 %collective-permute-start.5 = (s32[1]{0:T(128)}, s32[1]{0:T(128)}, u32[]{:S(2)}, u32[]{:S(2)}) collective-permute-start(s32[1]{0:T(128)} %get-tuple-element.8), channel_id=1, source_target_pairs={{0,24},{4,28},{8,16},{12,20},{16,8},{20,12},{24,0},{28,4},{1,25},{... | collective-permute-start | bytes 20 | tf_op jit(solution)/shard_map/ppermute | solution.py:62
  37.7 0.7 dynamic_update_slice.41
  38.4 0.0 collective-permute-done.1
  38.4 1.5 collective-permute-start.6
  39.8 0.7 dynamic_update_slice.42
  40.5 0.0 collective-permute-done.2
  40.5 0.7 dynamic_update_slice.43
  41.3 0.0 collective-permute-done.3
  41.3 0.7 dynamic_update_slice.44
  42.0 0.0 collective-permute-done.4
  42.0 0.7 dynamic_update_slice.45
  42.8 0.0 collective-permute-done.5
  42.8 0.8 dynamic_update_slice.46
  43.5 1.3 collective-permute-done.6
  44.9 0.7 dynamic_update_slice.47
  45.6 0.0 all-to-all-done
  45.6 1.3 convolution_convert_fusion.3
  47.0 9.7 %all_gather.3 = bf16[8,48,1280]{2,0,1:T(8,128)(2,1)S(1)} all-gather(bf16[8,12,1280]{2,0,1:T(8,128)(2,1)S(1)} %convolution_convert_fusion.3), channel_id=1, replica_groups=mesh['rep'=8,'tp'=4] {'tp'}, dimensions={1}, use_global_device_ids=true | all-gather | bytes 1228800 | tf_op jit(solution)/shard_map/all_gather | solution.py:78
  56.6 0.2 copy.16
  56.8 3.8 %fusion = bf16[384,1280]{1,0:T(8,128)(2,1)S(1)} fusion(bf16[384,1280]{1,0:T(8,128)(2,1)S(1)} %bitcast.31, bf16[1280,1280]{1,0:T(8,128)(2,1)S(1)} %copy-done.6, f32[384,1280]{1,0:T(8,128)} %fusion.34), kind=kOutput, calls=%fused_computation.5 | convolution fusion | flops 1267630080 | bytes 7208960 | tf_op jit(solution)/shard_map/dot_general | solution.py:89
  60.7 0.0 copy-done.2
  60.7 0.0 copy-start.7
  60.7 0.9 copy-done.7
  61.6 2.4 %convolution_convert_fusion.2 = bf16[384,1280]{1,0:T(8,128)(2,1)} fusion(bf16[384,1280]{1,0:T(8,128)(2,1)S(1)} %fusion, bf16[1280,1280]{1,0:T(8,128)(2,1)S(1)} %copy-done), kind=kOutput, calls=%fused_computation.6 | convolution fusion | flops 1258782720 | bytes 5242880 | tf_op jit(solution)/shard_map/dot_general | solution.py:93
  64.0 0.0 all-reduce.2.cloned.1.call-update
  64.1 0.0 reduce-scatter.3.cloned.1.call-start
  64.1 5.1 %convolution_convert_fusion.1 = bf16[1280,1280]{1,0:T(8,128)(2,1)} fusion(bf16[384,1280]{1,0:T(8,128)(2,1)} %copy-done.4, bf16[384,1280]{1,0:T(8,128)(2,1)} %copy-done.7), kind=kOutput, calls=%fused_computation.1 | convolution fusion | flops 1259929600 | bytes 5242880 | tf_op jit(solution)/shard_map/dot_general | solution.py:92
  69.2 0.0 reduce-scatter.3.cloned.1.call-update
  69.2 0.2 reduce-scatter.5.cloned.1.call-start
  69.5 5.5 %convolution_convert_fusion = bf16[1280,1280]{0,1:T(8,128)(2,1)} fusion(bf16[384,1280]{1,0:T(8,128)(2,1)} %bitcast.32, f32[384,1280]{1,0:T(8,128)} %fusion.34), kind=kOutput, calls=%fused_computation | convolution fusion | flops 1264353280 | bytes 6225920 | tf_op jit(solution)/shard_map/dot_general | solution.py:91
  75.0 0.0 reduce-scatter.5.cloned.1.call-update
  75.0 23.0 %all-reduce.2.cloned.1.call-done = bf16[384,1280]{1,0:T(8,128)(2,1)} async-done(((bf16[384,1280]{1,0:T(8,128)(2,1)}), bf16[384,1280]{1,0:T(8,128)(2,1)}) %all-reduce.2.cloned.1.call-update) | async-done | bytes 983056 | tf_op jit(solution)/shard_map/psum | solution.py:103
  98.1 2.6 %fusion.8 = (f32[1280]{0:T(1024)S(1)}, f32[384]{0:T(512)S(1)}, f32[384]{0:T(512)S(1)}) fusion(bf16[384,1280]{1,0:T(8,128)(2,1)} %all-reduce.2.cloned.1.call-done, bf16[8,48,1280]{2,1,0:T(8,128)(2,1)} %param.10, f32[384]{0:T(512)S(1)} %div.18, f32[384]{0:T(512)S(1)} %sqrt.6, f32[1280]{0:T(1024)S(1)} %copy-done.5), kind=kLoop, calls=%fused_computation.18 | loop fusion | flops 4913152 | bytes 1982464 | tf_op jit(solution)/shard_map/reduce_sum | solution.py:104
  100.7 2.1 fusion.6
  102.7 0.1 constant_dynamic-slice_fusion
  102.8 0.8 copy.22
  103.6 22.1 %psum.15 = f32[1280]{0:T(1024)} all-reduce(f32[1280]{0:T(1024)S(1)} %get-tuple-element.4), channel_id=1, replica_groups=mesh['rep'=8,'tp'=4] {'rep'}, use_global_device_ids=true, to_apply=%region_10.11 | all-reduce | flops 1280 | bytes 10240 | tf_op jit(solution)/shard_map/psum | solution.py:104
  125.7 18.1 %reduce-scatter.3.cloned.1.call-done = bf16[160,1280]{1,0:T(8,128)(2,1)} async-done(((bf16[1280,1280]{1,0:T(8,128)(2,1)}), bf16[160,1280]{1,0:T(8,128)(2,1)}) %reduce-scatter.3.cloned.1.call-update) | async-done | bytes 409616 | tf_op jit(solution)/shard_map/reduce_scatter | solution.py:95
  143.8 1.9 convert_element_type.63
  145.8 76.7 %reduce-scatter.5.cloned.1.call-done = bf16[1280,160]{0,1:T(8,128)(2,1)} async-done(((bf16[1280,1280]{0,1:T(8,128)(2,1)}), bf16[1280,160]{0,1:T(8,128)(2,1)}) %reduce-scatter.5.cloned.1.call-update) | async-done | bytes 409616 | tf_op jit(solution)/shard_map/reduce_scatter | solution.py:98
  222.4 1.9 convert_element_type.66
  (14 shorter events, 0.0 us)
Async XLA Ops:
  8.0 23.1 %copy-start = (bf16[1280,1280]{1,0:T(8,128)(2,1)S(1)}, bf16[1280,1280]{1,0:T(8,128)(2,1)}, u32[]{:S(2)}) copy-start(bf16[1280,1280]{1,0:T(8,128)(2,1)} %param.11) | copy-start | bytes 9830404
  8.0 21.5 %copy-start.5 = (f32[1280]{0:T(1024)S(1)}, f32[1280]{0:T(1024)}, u32[]{:S(2)}) copy-start(f32[1280]{0:T(1024)} %param.13) | copy-start | bytes 15364
  10.6 23.4 %collective-permute-start = (s32[1]{0:T(128)}, s32[1]{0:T(128)}, u32[]{:S(2)}, u32[]{:S(2)}) collective-permute-start(s32[1]{0:T(128)} %get-tuple-element.13), channel_id=1, source_target_pairs={{0,4},{4,0},{8,12},{12,8},{16,20},{20,16},{24,28},{28,24},{1,5},{5... | collective-permute-start | bytes 20 | tf_op jit(solution)/shard_map/ppermute | solution.py:62
  13.6 24.8 %collective-permute-start.1 = (s32[1]{0:T(128)}, s32[1]{0:T(128)}, u32[]{:S(2)}, u32[]{:S(2)}) collective-permute-start(s32[1]{0:T(128)} %get-tuple-element.12), channel_id=1, source_target_pairs={{0,8},{4,12},{8,0},{12,4},{16,24},{20,28},{24,16},{28,20},{1,9},{5... | collective-permute-start | bytes 20 | tf_op jit(solution)/shard_map/ppermute | solution.py:62
  15.1 25.4 %collective-permute-start.2 = (s32[1]{0:T(128)}, s32[1]{0:T(128)}, u32[]{:S(2)}, u32[]{:S(2)}) collective-permute-start(s32[1]{0:T(128)} %get-tuple-element.11), channel_id=1, source_target_pairs={{0,12},{4,8},{8,4},{12,0},{16,28},{20,24},{24,20},{28,16},{1,13},{... | collective-permute-start | bytes 20 | tf_op jit(solution)/shard_map/ppermute | solution.py:62
  15.1 26.1 %collective-permute-start.3 = (s32[1]{0:T(128)}, s32[1]{0:T(128)}, u32[]{:S(2)}, u32[]{:S(2)}) collective-permute-start(s32[1]{0:T(128)} %get-tuple-element.10), channel_id=1, source_target_pairs={{0,16},{4,20},{8,24},{12,28},{16,0},{20,4},{24,8},{28,12},{1,17},{... | collective-permute-start | bytes 20 | tf_op jit(solution)/shard_map/ppermute | solution.py:62
  18.1 23.9 %collective-permute-start.4 = (s32[1]{0:T(128)}, s32[1]{0:T(128)}, u32[]{:S(2)}, u32[]{:S(2)}) collective-permute-start(s32[1]{0:T(128)} %get-tuple-element.9), channel_id=1, source_target_pairs={{0,20},{4,16},{8,28},{12,24},{16,4},{20,0},{24,12},{28,8},{1,21},{... | collective-permute-start | bytes 20 | tf_op jit(solution)/shard_map/ppermute | solution.py:62
  21.4 24.2 %all-to-all-start = ((bf16[8,12,1280]{2,1,0:T(8,128)(2,1)}), bf16[8,12,1280]{2,1,0:T(8,128)(2,1)}, u32[]{:S(2)}, u32[]{:S(2)}) async-start(bf16[8,12,1280]{2,1,0:T(8,128)(2,1)} %copy.14), calls=%async_computation | async-start | bytes 655360 | tf_op jit(solution)/shard_map/all_to_all | solution.py:75
  26.3 71.8 %all-reduce.2.cloned.1.call-start = ((), (), s32[]{:S(2)}) async-start(), calls=%async_computation.3 | async-start | bytes 1966080 | tf_op jit(solution)/shard_map/psum | solution.py:103
  31.1 2.8 %copy-start.4 = (bf16[384,1280]{1,0:T(8,128)(2,1)}, bf16[384,1280]{1,0:T(8,128)(2,1)S(1)}, u32[]{:S(2)}) copy-start(bf16[384,1280]{1,0:T(8,128)(2,1)S(1)} %multiply_convert_fusion.1) | copy-start | bytes 2949124
  33.9 8.8 %collective-permute-start.5 = (s32[1]{0:T(128)}, s32[1]{0:T(128)}, u32[]{:S(2)}, u32[]{:S(2)}) collective-permute-start(s32[1]{0:T(128)} %get-tuple-element.8), channel_id=1, source_target_pairs={{0,24},{4,28},{8,16},{12,20},{16,8},{20,12},{24,0},{28,4},{1,25},{... | collective-permute-start | bytes 20 | tf_op jit(solution)/shard_map/ppermute | solution.py:62
  38.4 6.5 %collective-permute-start.6 = (s32[1]{0:T(128)}, s32[1]{0:T(128)}, u32[]{:S(2)}, u32[]{:S(2)}) collective-permute-start(s32[1]{0:T(128)} %get-tuple-element.7), channel_id=1, source_target_pairs={{0,28},{4,24},{8,20},{12,16},{16,12},{20,8},{24,4},{28,0},{1,29},{... | collective-permute-start | bytes 20 | tf_op jit(solution)/shard_map/ppermute | solution.py:62
  45.6 11.2 %copy-start.6 = (bf16[1280,1280]{1,0:T(8,128)(2,1)S(1)}, bf16[1280,1280]{1,0:T(8,128)(2,1)}, u32[]{:S(2)}) copy-start(bf16[1280,1280]{1,0:T(8,128)(2,1)} %param.12) | copy-start | bytes 9830404
  56.8 3.9 %copy-start.2 = (bf16[8,48,1280]{2,1,0:T(8,128)(2,1)}, bf16[8,48,1280]{2,1,0:T(8,128)(2,1)S(1)}, u32[]{:S(2)}) copy-start(bf16[8,48,1280]{2,1,0:T(8,128)(2,1)S(1)} %copy.16) | copy-start | bytes 2949124
  60.7 1.0 copy-start.7
  64.1 79.7 %reduce-scatter.3.cloned.1.call-start = ((), (), s32[]{:S(2)}) async-start(), calls=%async_computation.4 | async-start | bytes 3686400 | tf_op jit(solution)/shard_map/reduce_scatter | solution.py:95
  69.2 153.2 %reduce-scatter.5.cloned.1.call-start = ((), (), s32[]{:S(2)}) async-start(), calls=%async_computation.5 | async-start | bytes 3686400 | tf_op jit(solution)/shard_map/reduce_scatter | solution.py:98
  98.1 2.6 %copy-start.1 = (bf16[8,48,1280]{2,1,0:T(8,128)(2,1)S(1)}, bf16[8,48,1280]{2,1,0:T(8,128)(2,1)}, u32[]{:S(2)}) copy-start(bf16[8,48,1280]{2,1,0:T(8,128)(2,1)} %param.10) | copy-start | bytes 2949124
  98.1 2.6 %copy-start.3 = (bf16[8,48,1280]{2,1,0:T(8,128)(2,1)S(1)}, bf16[8,48,1280]{2,1,0:T(8,128)(2,1)}, u32[]{:S(2)}) copy-start(bf16[8,48,1280]{2,1,0:T(8,128)(2,1)} %copy-done.2) | copy-start | bytes 2949124
Sparse Core Ops, SparseCore 0:
  64.2 33.8 all-reduce.1
Sparse Core Ops, SparseCore 1:
  69.3 74.4 reduce-scatter.2
  147.3 75.1 reduce-scatter.4
